TPU v7x, 32 devices: a whole 2x2x4 slice. The times are simulated.
32 devices in a mesh: seq: 8 (over z, y), ch: 4 (over x, core).
Axes of the slice: x: 2, y: 2, z: 4, core: 2. Of those that a mesh axis runs over, the one named last changes fastest.
Arguments:
- inputs: bfloat16 [1024, 4096], P('seq', 'ch'), may hold values from -6 to 6
- gate_values: bfloat16 [1024, 4096], P('seq', 'ch'), may hold values from -6 to 6
- grad_out: bfloat16 [1024, 4096], P('seq', 'ch'), may hold values from -6 to 6
- first_weight: float32 [32, 256], replicated, may hold values from -4 to 4
- first_bias: float32 [256], replicated, may hold values from -3.140625 to 3.140625
- second_weight: float32 [256, 256], replicated, may hold values from -0.75 to 0.75
- second_bias: float32 [256], replicated, may hold values from -3.140625 to 3.140625
- out_weight: float32 [256, 4096], P(None, 'ch'), may hold values from -0.0546875 to 0.0546875
- decay_rates: float32 [4096], P('ch'), as said below
- mask_lengths: int32 [4096], P('ch'), may hold values from 1 to 512, as said below
Outputs:
- grad_inputs: bfloat16 [1024, 4096], P('seq', 'ch')
- grad_gates: bfloat16 [1024, 4096], P('seq', 'ch')
- grad_first_weight: float32 [32, 256], replicated
- grad_first_bias: float32 [256], replicated
- grad_second_weight: float32 [256, 256], replicated
- grad_second_bias: float32 [256], replicated
- grad_out_weight: float32 [256, 4096], P(None, 'ch')
Inputs may be any that keep to these rules, and one draw needn't show every extreme that they name: `mask_lengths`: each channel's decay-mask length in lags; in every aligned group of 32 channels at least one channel has exactly 512. `decay_rates`: positive decay rates between 1 / 5120 and 1 / 40.
All inputs are finite; a program needn't handle non-finite values.
Results may differ from a plain program's by a relative error of at most 0.013.
Values may be sent and summed in bfloat16 or wider, within the bound.
A program may use at most 128 MiB of HBM per device.

v0:
```python
import math

import jax
import jax.numpy as jnp
import functools

import numpy as np
from jax import lax
from jax.experimental import pallas as pl
from jax.experimental.pallas import tpu as pltpu
from jax.sharding import PartitionSpec as P

SPAN = 4


FULL_PRECISION = lax.Precision.HIGHEST


def passed_along(value, axis, steps):
    count = lax.axis_size(axis)
    pairs = [(source, (source + steps) % count) for source in range(count)]
    return lax.ppermute(value, axis, pairs)


def angle_table(first_index, second_index, period):
    product = first_index[:, None] * second_index[None, :] % period
    return 2.0 * math.pi / period * product.astype(jnp.float32)


def lag_features(lag_count, feature_count):
    lag_index = jnp.arange(lag_count, dtype=jnp.int32)
    band_index = jnp.arange(feature_count // 2, dtype=jnp.int32) + 1
    phases = angle_table(lag_index, band_index, 2 * feature_count)
    return jnp.concatenate([jnp.cos(phases), jnp.sin(phases)], axis=1)


def split_table(table):
    upper_part = table.astype(jnp.bfloat16)
    lower_part = (table - upper_part.astype(jnp.float32)).astype(jnp.bfloat16)
    return (upper_part, lower_part)


def transform_tables(shard_rows):
    period = 2 * shard_rows
    frequency = jnp.arange(shard_rows + 1, dtype=jnp.int32)
    position = jnp.arange(shard_rows, dtype=jnp.int32)
    bin_weight = jnp.where((frequency == 0) | (frequency == shard_rows), 1.0, 2.0).astype(
        jnp.float32
    )
    forward_angles = angle_table(frequency, position, period)
    mirror_angles = angle_table(frequency, shard_rows - 1 - position, period)
    back_angles = angle_table(position + shard_rows, frequency, period)
    mirror_back = angle_table(2 * shard_rows - 1 - position, frequency, period)
    front_table = jnp.stack([jnp.cos(forward_angles), -jnp.sin(forward_angles)])
    mirror_table = jnp.stack([jnp.cos(mirror_angles), -jnp.sin(mirror_angles)])
    back_plain = jnp.stack([jnp.cos(back_angles), -jnp.sin(back_angles)]) / period
    back_table = back_plain * bin_weight[None, None, :]
    mirror_out = jnp.stack([jnp.cos(mirror_back), -jnp.sin(mirror_back)]) * (
        bin_weight[None, None, :] / period
    )
    fold_table = front_table * bin_weight[None, :, None]
    parity = (1.0 - 2.0 * (frequency % 2).astype(jnp.float32))[None, :, None]
    return (front_table, mirror_table, back_plain, back_table, mirror_out, fold_table, parity)


def spectrum(table_in, signal):
    return jnp.einsum("kfs,sc->kfc", table_in, signal, precision=FULL_PRECISION)


def sample_spectrum(table_pair, signal):
    upper_term = jnp.einsum(
        "kfs,sc->kfc", table_pair[0], signal, preferred_element_type=jnp.float32
    )
    lower_term = jnp.einsum(
        "kfs,sc->kfc", table_pair[1], signal, preferred_element_type=jnp.float32
    )
    return upper_term + lower_term


def sample_pullback(table_pair, signal):
    upper_term = jnp.einsum(
        "ksf,sc->kfc", table_pair[0], signal, preferred_element_type=jnp.float32
    )
    lower_term = jnp.einsum(
        "ksf,sc->kfc", table_pair[1], signal, preferred_element_type=jnp.float32
    )
    return upper_term + lower_term


def complex_product(left_factor, right_factor):
    real_part = left_factor[0] * right_factor[0] - left_factor[1] * right_factor[1]
    imag_part = left_factor[0] * right_factor[1] + left_factor[1] * right_factor[0]
    return jnp.stack([real_part, imag_part])


def conjugate_product(left_factor, right_factor):
    real_part = left_factor[0] * right_factor[0] + left_factor[1] * right_factor[1]
    imag_part = left_factor[1] * right_factor[0] - left_factor[0] * right_factor[1]
    return jnp.stack([real_part, imag_part])


def weighted_sum(filter_mixes, spectra_items):
    accumulated = complex_product(filter_mixes[0], spectra_items[0])
    for offset in range(1, len(filter_mixes)):
        accumulated = accumulated + complex_product(filter_mixes[offset], spectra_items[offset])
    return accumulated


def per_device(
    inputs,
    gate_values,
    grad_out,
    first_weight,
    first_bias,
    second_weight,
    second_bias,
    out_weight,
    decay_rates,
    mask_lengths,
):
    shard_rows = inputs.shape[0]
    window = SPAN * shard_rows
    front_table, mirror_table, back_plain, back_table, mirror_out, fold_table, parity = (
        transform_tables(shard_rows)
    )
    front_pair = split_table(front_table)
    mirror_pair = split_table(mirror_table)
    pull_pair = split_table(back_plain)
    features = lag_features(window, first_weight.shape[0])
    pre_first = jnp.dot(features, first_weight, precision=FULL_PRECISION) + first_bias
    hidden_one = jnp.sin(pre_first)
    pre_second = jnp.dot(hidden_one, second_weight, precision=FULL_PRECISION) + second_bias
    hidden_two = jnp.sin(pre_second)
    lag_index = jnp.arange(window, dtype=jnp.int32)
    envelope = jnp.exp(-decay_rates[None, :] * lag_index.astype(jnp.float32)[:, None]) * (
        lag_index[:, None] < mask_lengths[None, :]
    ).astype(jnp.float32)
    filter_taps = jnp.dot(hidden_two, out_weight, precision=FULL_PRECISION) * envelope
    block_spectra = [
        spectrum(front_table, filter_taps[block * shard_rows : (block + 1) * shard_rows])
        for block in range(SPAN)
    ]
    filter_mixes = []
    for offset in range(SPAN + 1):
        if offset == 0:
            mixed = parity * block_spectra[0]
        elif offset == SPAN:
            mixed = block_spectra[SPAN - 1]
        else:
            mixed = block_spectra[offset - 1] + parity * block_spectra[offset]
        filter_mixes.append(mixed)
    carried = (grad_out.astype(jnp.float32) * gate_values.astype(jnp.float32)).astype(jnp.bfloat16)
    earlier_spectra = [sample_spectrum(front_pair, inputs)]
    later_spectra = [sample_spectrum(mirror_pair, carried)]
    for offset in range(1, SPAN + 1):
        earlier = passed_along(inputs, "seq", offset)
        later = passed_along(carried, "seq", -offset)
        earlier_spectra.append(sample_spectrum(front_pair, earlier))
        later_spectra.append(sample_spectrum(mirror_pair, later))
    convolved = jnp.einsum(
        "ksf,kfc->sc",
        back_table,
        weighted_sum(filter_mixes, earlier_spectra),
        precision=FULL_PRECISION,
    )
    grad_gates = (grad_out.astype(jnp.float32) * convolved).astype(jnp.bfloat16)
    grad_inputs = jnp.einsum(
        "ksf,kfc->sc",
        mirror_out,
        weighted_sum(filter_mixes, later_spectra),
        precision=FULL_PRECISION,
    ).astype(jnp.bfloat16)
    pulled = sample_pullback(pull_pair, carried)
    grad_mixes = [conjugate_product(pulled, spectra_item) for spectra_item in earlier_spectra]
    pieces = []
    for block in range(SPAN):
        grad_block = parity * grad_mixes[block] + grad_mixes[block + 1]
        pieces.append(jnp.einsum("kfs,kfc->sc", fold_table, grad_block, precision=FULL_PRECISION))
    tap_terms = jnp.concatenate(pieces, axis=0)
    grad_scale = 1.0 / math.sqrt(lax.axis_size("seq") * shard_rows * window)
    tap_sums = lax.psum(tap_terms, "seq")
    grad_taps = tap_sums * envelope * grad_scale
    grad_out_weight = jnp.dot(hidden_two.T, grad_taps, precision=FULL_PRECISION)
    unit_grad = lax.psum(
        jnp.dot(grad_taps, out_weight.T, precision=FULL_PRECISION).astype(jnp.bfloat16), "ch"
    ).astype(jnp.float32)
    grad_two = unit_grad * jnp.cos(pre_second)
    grad_second_weight = jnp.dot(hidden_one.T, grad_two, precision=FULL_PRECISION)
    grad_second_bias = jnp.sum(grad_two, axis=0)
    grad_one = jnp.dot(grad_two, second_weight.T, precision=FULL_PRECISION) * jnp.cos(pre_first)
    grad_first_weight = jnp.dot(features.T, grad_one, precision=FULL_PRECISION)
    grad_first_bias = jnp.sum(grad_one, axis=0)
    return (
        grad_inputs,
        grad_gates,
        grad_first_weight,
        grad_first_bias,
        grad_second_weight,
        grad_second_bias,
        grad_out_weight,
    )


MESH = pl.DeviceIdType.MESH


def bf(value):
    return value.astype(jnp.bfloat16)


def dot(left, right, dims=((1,), (0,)), precision=None):
    return lax.dot_general(
        left, right, (dims, ((), ())), precision=precision, preferred_element_type=jnp.float32
    )


def packed_table(tokens):
    half = tokens // 2
    freq = np.arange(half)[:, None]
    time = np.arange(tokens)[None, :]
    angles = 2.0 * np.pi / tokens * (freq * time % tokens)
    lower = -np.sin(angles)
    lower[0] = 1.0 - 2.0 * (np.arange(tokens) % 2)
    return np.concatenate([np.cos(angles), lower]).astype(np.float32)


def exchange_kernel(
    sizes, x_ref, gate_ref, gout_ref, w1_ref, b1_ref, w2_ref, b2_ref, decay_ref, mask_ref,
    feat_ref, featt_ref, table_hbm, ow_hbm,
    gi_ref, gg_ref, gw1_ref, gb1_ref, gw2_ref, gb2_ref, gow_ref,
    table, turned, ow, carried, xc, conv_in, taps, env, spec, tspec, prod, back, sums,
    gts, gtall, units, send_sem, recv_sem, usend, urecv, local_sem,
):
    n, m, rows, width, window, period = sizes
    tokens = n * rows
    half = tokens // 2
    me = lax.axis_index("seq")
    mine = lax.axis_index("ch")
    table_copy = pltpu.make_async_copy(table_hbm, table, local_sem.at[0])
    table_copy.start()
    ow_copy = pltpu.make_async_copy(ow_hbm, ow, local_sem.at[1])
    ow_copy.start()
    carried[...] = bf(gout_ref[...].astype(jnp.float32) * gate_ref[...].astype(jnp.float32))
    order = sorted(range(1, n), key=lambda step: -min(step, n - step))
    peers = {step: lax.rem(me + step, n) for step in order}
    others = {step: lax.rem(mine + step, m) for step in range(1, m)}

    barrier = pltpu.get_barrier_semaphore()
    for step in order:
        pl.semaphore_signal(barrier, inc=1, device_id={"seq": peers[step]}, device_id_type=MESH)
    for step in range(1, m):
        pl.semaphore_signal(barrier, inc=1, device_id={"ch": others[step]}, device_id_type=MESH)
    pl.semaphore_wait(barrier, n + m - 2)

    own_rows = pl.ds(pl.multiple_of(me * rows, rows), rows)
    own_cols = pl.ds(pl.multiple_of(me * width, width), width)

    def send(kind, step, source, target):
        copy = pltpu.make_async_remote_copy(
            src_ref=source, dst_ref=target,
            send_sem=send_sem.at[kind, step], recv_sem=recv_sem.at[kind, step],
            device_id={"seq": peers[step]}, device_id_type=MESH,
        )
        copy.start()
        return copy

    arriving = []
    for kind, source in ((0, x_ref), (1, carried)):
        for step in order:
            cols = pl.ds(pl.multiple_of(peers[step] * width, width), width)
            arriving.append(
                send(kind, step, source.at[:, cols], xc.at[own_rows, pl.ds(kind * width, width)])
            )
    xc[own_rows, 0:width] = x_ref[:, own_cols]
    xc[own_rows, width : 2 * width] = carried[:, own_cols]

    full = lax.Precision.HIGHEST
    pre_one = dot(feat_ref[...], w1_ref[...], precision=full) + b1_ref[...]
    h_one = jnp.sin(pre_one)
    slope_one = jnp.cos(pre_one)
    pre_two = dot(h_one, w2_ref[...], precision=full) + b2_ref[...]
    h_two = jnp.sin(pre_two)
    slope_two = jnp.cos(pre_two)
    ow_copy.wait()
    base = dot(h_two, ow[:, own_cols], precision=full)
    decay = decay_ref[:, own_cols]
    lengths = mask_ref[:, own_cols]
    for block in range(window // period):
        lag = lax.broadcasted_iota(jnp.int32, (period, width), 0) + block * period
        part = jnp.where(lag < lengths, jnp.exp(-decay * lag.astype(jnp.float32)), 0.0)
        env[pl.ds(block * period, period), :] = part
        taps[pl.ds(block * period, period), :] = bf(base * part)
    table_copy.wait()

    @pl.loop(0, tokens // 256)
    def _(i):
        piece = pl.ds(pl.multiple_of(i * 256, 256), 256)
        tspec[piece, :] = dot(table[piece, 0:window], taps[...])
        turned[:, piece] = table[piece, :].T

    h_one_t = bf(h_one.T)
    h_two_t = bf(h_two.T)
    for copy in arriving:
        copy.wait()

    @pl.loop(0, tokens // 256)
    def _(i):
        piece = pl.ds(pl.multiple_of(i * 256, 256), 256)
        spec[piece, :] = dot(table[piece, :], xc[...])

    @pl.loop(0, half // 64)
    def _(i):
        upper = pl.ds(pl.multiple_of(i * 64, 64), 64)
        lower = pl.ds(pl.multiple_of(half + i * 64, 64), 64)
        first = (lax.broadcasted_iota(jnp.int32, (64, width), 0) + i * 64) == 0
        weight = jnp.where(first, 1.0 / tokens, 2.0 / tokens)
        xr, xi = spec[upper, 0:width], spec[lower, 0:width]
        cr, ci = spec[upper, width : 2 * width], spec[lower, width : 2 * width]
        hr, hi = tspec[upper, :], tspec[lower, :]
        cx, hc, hx = ci * xi, hi * ci, hi * xi
        ts_r = cr * xr + jnp.where(first, 0.0, cx)
        ts_i = jnp.where(first, cx, ci * xr - cr * xi)
        gi_r = hr * cr + jnp.where(first, 0.0, hc)
        gi_i = jnp.where(first, hc, hr * ci - hi * cr)
        cv_r = hr * xr - jnp.where(first, 0.0, hx)
        cv_i = jnp.where(first, hx, hr * xi + hi * xr)
        for at, (real, imag) in enumerate(((ts_r, ts_i), (gi_r, gi_i), (cv_r, cv_i))):
            cols = slice(at * width, (at + 1) * width)
            prod[upper, cols] = bf(real * weight)
            prod[lower, cols] = bf(imag * weight)

    @pl.loop(0, window // 256)
    def _(i):
        piece = pl.ds(pl.multiple_of(i * 256, 256), 256)
        sums[piece, :] = dot(turned[piece, :], prod[:, 0:width])

    folded = sums[0:period, :] * env[0:period, :]
    for block in range(1, window // period):
        piece = pl.ds(block * period, period)
        folded = folded + sums[piece, :] * env[piece, :]
    folded = bf(folded * (1.0 / math.sqrt(tokens * window)))
    gts[...] = folded
    gtall[:, own_cols] = folded
    gathering = [send(2, step, gts, gtall.at[:, own_cols]) for step in order]

    @pl.loop(0, tokens // 256)
    def _(i):
        piece = pl.ds(pl.multiple_of(i * 256, 256), 256)
        back[piece, :] = bf(dot(turned[piece, :], prod[:, width : 3 * width]))

    returning = []
    for step in order:
        piece = pl.ds(pl.multiple_of(peers[step] * rows, rows), rows)
        returning.append(send(3, step, back.at[piece, pl.ds(0, width)], gi_ref.at[:, own_cols]))
        returning.append(
            send(4, step, back.at[piece, pl.ds(width, width)], conv_in.at[:, own_cols])
        )
    gi_ref[:, own_cols] = back[own_rows, 0:width]
    conv_in[:, own_cols] = back[own_rows, width : 2 * width]

    for copy in gathering:
        copy.wait()
    units[mine] = bf(dot(gtall[...], bf(ow[...]), ((1,), (1,))))
    crossing = []
    for step in range(1, m):
        copy = pltpu.make_async_remote_copy(
            src_ref=units.at[mine], dst_ref=units.at[mine],
            send_sem=usend.at[step], recv_sem=urecv.at[step],
            device_id={"ch": others[step]}, device_id_type=MESH,
        )
        copy.start()
        crossing.append(copy)
    gow_ref[...] = dot(h_two_t, gtall[...])
    for copy in crossing:
        copy.wait()
    unit = units[0].astype(jnp.float32)
    for other in range(1, m):
        unit = unit + units[other].astype(jnp.float32)
    grad_two = unit * slope_two
    gw2_ref[...] = dot(h_one_t, bf(grad_two))
    gb2_ref[...] = jnp.sum(grad_two, axis=0, keepdims=True)
    grad_one = dot(bf(grad_two), bf(w2_ref[...]), ((1,), (1,))) * slope_one
    gw1_ref[...] = dot(bf(featt_ref[...]), bf(grad_one))
    gb1_ref[...] = jnp.sum(grad_one, axis=0, keepdims=True)
    for copy in returning:
        copy.wait()
    gg_ref[...] = bf(gout_ref[...].astype(jnp.float32) * conv_in[...].astype(jnp.float32))


def exchanged(
    mesh_shape, inputs, gate_values, grad_out, first_weight, first_bias, second_weight,
    second_bias, out_weight, decay_rates, mask_lengths,
):
    n, m = mesh_shape["seq"], mesh_shape["ch"]
    rows, channels = inputs.shape
    width = channels // n
    window = SPAN * rows
    emb, units = first_weight.shape
    period = 2 * emb
    tokens = n * rows
    angles = (
        2.0 * np.pi / period
        * (np.arange(period)[:, None] * (np.arange(emb // 2)[None, :] + 1) % period)
    )
    features = np.concatenate([np.cos(angles), np.sin(angles)], axis=1).astype(np.float32)
    f32, b16 = jnp.float32, jnp.bfloat16
    vmem = pl.BlockSpec(memory_space=pltpu.VMEM)
    anywhere = pl.BlockSpec(memory_space=pl.ANY)
    shape = jax.ShapeDtypeStruct
    sem = pltpu.SemaphoreType.DMA
    outs = pl.pallas_call(
        functools.partial(exchange_kernel, (n, m, rows, width, window, period)),
        out_shape=(
            shape((rows, channels), b16), shape((rows, channels), b16),
            shape((emb, units), f32), shape((1, units), f32),
            shape((units, units), f32), shape((1, units), f32),
            shape((units, channels), f32),
        ),
        in_specs=[vmem] * 11 + [anywhere] * 2,
        out_specs=(vmem,) * 7,
        scratch_shapes=[
            pltpu.VMEM((tokens, tokens), b16), pltpu.VMEM((tokens, tokens), b16),
            pltpu.VMEM((units, channels), f32), pltpu.VMEM((rows, channels), b16),
            pltpu.VMEM((tokens, 2 * width), b16), pltpu.VMEM((rows, channels), b16),
            pltpu.VMEM((window, width), b16), pltpu.VMEM((window, width), f32),
            pltpu.VMEM((tokens, 2 * width), f32), pltpu.VMEM((tokens, width), f32),
            pltpu.VMEM((tokens, 3 * width), b16), pltpu.VMEM((tokens, 2 * width), b16),
            pltpu.VMEM((window, width), f32),
            pltpu.VMEM((period, width), b16), pltpu.VMEM((period, channels), b16),
            pltpu.VMEM((m, period, units), b16),
            sem((5, n)), sem((5, n)), sem((m,)), sem((m,)), sem((2,)),
        ],
        compiler_params=pltpu.CompilerParams(
            collective_id=0, has_side_effects=True, vmem_limit_bytes=48 * 1024 * 1024
        ),
        name="exchange",
    )(
        inputs, gate_values, grad_out, first_weight, first_bias[None], second_weight,
        second_bias[None], decay_rates[None], mask_lengths[None],
        jnp.asarray(features), jnp.asarray(features.T.copy()),
        jnp.asarray(packed_table(tokens), dtype=b16), out_weight,
    )
    grad_in, gates, gw1, gb1, gw2, gb2, gow = outs
    return grad_in, gates, gw1, gb1[0], gw2, gb2[0], gow


def solution(mesh):
    def body(*arrays):
        rows, channels = arrays[0].shape
        fits = channels == 128 * mesh.shape["seq"] and rows % 128 == 0
        if fits:
            return exchanged(mesh.shape, *arrays)
        return per_device(*arrays)

    in_specs = (
        P("seq", "ch"),
        P("seq", "ch"),
        P("seq", "ch"),
        P(),
        P(),
        P(),
        P(),
        P(None, "ch"),
        P("ch"),
        P("ch"),
    )
    out_specs = (P("seq", "ch"), P("seq", "ch"), P(), P(), P(), P(), P(None, "ch"))
    return jax.shard_map(
        body, mesh=mesh, in_specs=in_specs, out_specs=out_specs, check_vma=False
    )
```

profile of v0, /device:TPU:0, one launch (start us, length us, event | category | flops | bytes accessed | tf_op | source)
XLA Modules:
  0.0 52.3 jit_solution(17912763749855299767)
XLA Ops:
  0.6 0.0 copy-start
  0.6 1.6 %copy-done = bf16[1024,1024]{1,0:T(8,128)(2,1)S(1)} copy-done((bf16[1024,1024]{1,0:T(8,128)(2,1)S(1)}, bf16[1024,1024]{1,0:T(8,128)(2,1)}, u32[]{:S(2)}) %copy-start) | copy-done | bytes 2097176
  2.2 0.0 copy-start.1
  2.2 1.2 %copy-done.1 = f32[256,1024]{1,0:T(8,128)S(1)} copy-done((f32[256,1024]{1,0:T(8,128)S(1)}, f32[256,1024]{1,0:T(8,128)}, u32[]{:S(2)}) %copy-start.1) | copy-done | bytes 1048600
  3.5 0.0 copy-start.2
  3.5 0.9 %copy-done.2 = bf16[128,1024]{1,0:T(8,128)(2,1)S(1)} copy-done((bf16[128,1024]{1,0:T(8,128)(2,1)S(1)}, bf16[128,1024]{1,0:T(8,128)(2,1)}, u32[]{:S(2)}) %copy-start.2) | copy-done | bytes 262168
  4.4 0.0 copy-start.3
  4.4 0.9 %copy-done.3 = bf16[128,1024]{1,0:T(8,128)(2,1)S(1)} copy-done((bf16[128,1024]{1,0:T(8,128)(2,1)S(1)}, bf16[128,1024]{1,0:T(8,128)(2,1)}, u32[]{:S(2)}) %copy-start.3) | copy-done | bytes 262168
  5.4 0.0 copy-start.4
  5.4 0.9 %copy-done.4 = bf16[128,1024]{1,0:T(8,128)(2,1)S(1)} copy-done((bf16[128,1024]{1,0:T(8,128)(2,1)S(1)}, bf16[128,1024]{1,0:T(8,128)(2,1)}, u32[]{:S(2)}) %copy-start.4) | copy-done | bytes 262168
  6.3 0.0 copy-start.5
  6.3 0.9 %copy-done.5 = f32[256,256]{1,0:T(8,128)S(1)} copy-done((f32[256,256]{1,0:T(8,128)S(1)}, f32[256,256]{1,0:T(8,128)}, u32[]{:S(2)}) %copy-start.5) | copy-done | bytes 262168
  7.3 0.0 copy-start.6
  7.3 0.8 %copy-done.6 = f32[32,256]{1,0:T(8,128)S(1)} copy-done((f32[32,256]{1,0:T(8,128)S(1)}, f32[32,256]{1,0:T(8,128)}, u32[]{:S(2)}) %copy-start.6) | copy-done | bytes 32792
  8.0 0.0 copy-start.7
  8.0 0.8 %copy-done.7 = f32[64,32]{1,0:T(8,128)S(1)} copy-done((f32[64,32]{1,0:T(8,128)S(1)}, f32[64,32]{1,0:T(8,128)}, u32[]{:S(2)}) %copy-start.7) | copy-done | bytes 8216
  8.8 0.0 copy-start.8
  8.8 0.7 %copy-done.8 = f32[32,64]{1,0:T(8,128)S(1)} copy-done((f32[32,64]{1,0:T(8,128)S(1)}, f32[32,64]{1,0:T(8,128)}, u32[]{:S(2)}) %copy-start.8) | copy-done | bytes 8216
  9.5 0.7 %copy-done.9 = f32[1024]{0:T(1024)S(1)} copy-done((f32[1024]{0:T(1024)S(1)}, f32[1024]{0:T(1024)}, u32[]{:S(2)}) %copy-start.9) | copy-done | bytes 4120
  10.2 0.0 copy-start.10
  10.2 0.7 %copy-done.10 = s32[1024]{0:T(1024)S(1)} copy-done((s32[1024]{0:T(1024)S(1)}, s32[1024]{0:T(1024)}, u32[]{:S(2)}) %copy-start.10) | copy-done | bytes 4120
  10.9 0.0 copy-start.11
  10.9 0.7 %copy-done.11 = f32[256]{0:T(256)S(1)} copy-done((f32[256]{0:T(256)S(1)}, f32[256]{0:T(256)}, u32[]{:S(2)}) %copy-start.11) | copy-done | bytes 1048
  11.5 0.7 %copy-done.12 = f32[256]{0:T(256)S(1)} copy-done((f32[256]{0:T(256)S(1)}, f32[256]{0:T(256)}, u32[]{:S(2)}) %copy-start.12) | copy-done | bytes 1048
  12.2 35.2 %exchange.1 = (bf16[128,1024]{1,0:T(8,128)(2,1)S(1)}, bf16[128,1024]{1,0:T(8,128)(2,1)S(1)}, f32[32,256]{1,0:T(8,128)S(1)}, f32[1,256]{1,0:T(1,128)S(1)}, f32[25...) custom-call(bf16[128,1024]{1,0:T(8,128)(2,1)S(1)} %copy-done.2, bf16[128,1024]{1,0:T(8,128)(2,1)S(1)} %copy-done.3, ...), custom_call_target="tpu_custom_call" | custom-call | tf_op jit(solution)/shard_map/exchange/pallas_call | solution.py:411
  47.5 0.7 %copy.27 = bf16[128,1024]{1,0:T(8,128)(2,1)} copy(bf16[128,1024]{1,0:T(8,128)(2,1)S(1)} %get-tuple-element.28) | data formatting | bytes 524288
  48.2 0.7 %copy.28 = bf16[128,1024]{1,0:T(8,128)(2,1)} copy(bf16[128,1024]{1,0:T(8,128)(2,1)S(1)} %get-tuple-element.29) | data formatting | bytes 524288
  48.9 0.6 %copy.29 = f32[32,256]{1,0:T(8,128)} copy(f32[32,256]{1,0:T(8,128)S(1)} %get-tuple-element.30) | data formatting | bytes 65536
  49.5 0.6 %copy.30 = f32[256]{0:T(256)} copy(f32[256]{0:T(256)S(1)} %bitcast.9) | data formatting | bytes 2048
  50.1 0.7 %copy.31 = f32[256,256]{1,0:T(8,128)} copy(f32[256,256]{1,0:T(8,128)S(1)} %get-tuple-element.32) | data formatting | bytes 524288
  50.8 0.6 %copy.32 = f32[256]{0:T(256)} copy(f32[256]{0:T(256)S(1)} %bitcast.8) | data formatting | bytes 2048
  51.3 1.0 %copy.33 = f32[256,1024]{1,0:T(8,128)} copy(f32[256,1024]{1,0:T(8,128)S(1)} %get-tuple-element.34) | data formatting | bytes 2097152
  (2 shorter events, 0.0 us)
Async XLA Ops:
  0.6 1.6 %copy-start = (bf16[1024,1024]{1,0:T(8,128)(2,1)S(1)}, bf16[1024,1024]{1,0:T(8,128)(2,1)}, u32[]{:S(2)}) copy-start(bf16[1024,1024]{1,0:T(8,128)(2,1)} %constant.8.clone.table_hbm) | copy-start | bytes 6291460
  2.2 1.2 %copy-start.1 = (f32[256,1024]{1,0:T(8,128)S(1)}, f32[256,1024]{1,0:T(8,128)}, u32[]{:S(2)}) copy-start(f32[256,1024]{1,0:T(8,128)} %ow_hbm.1) | copy-start | bytes 3145732
  3.5 0.9 %copy-start.2 = (bf16[128,1024]{1,0:T(8,128)(2,1)S(1)}, bf16[128,1024]{1,0:T(8,128)(2,1)}, u32[]{:S(2)}) copy-start(bf16[128,1024]{1,0:T(8,128)(2,1)} %x_ref.1) | copy-start | bytes 786436
  4.4 0.9 %copy-start.3 = (bf16[128,1024]{1,0:T(8,128)(2,1)S(1)}, bf16[128,1024]{1,0:T(8,128)(2,1)}, u32[]{:S(2)}) copy-start(bf16[128,1024]{1,0:T(8,128)(2,1)} %gate_ref.1) | copy-start | bytes 786436
  5.4 0.9 %copy-start.4 = (bf16[128,1024]{1,0:T(8,128)(2,1)S(1)}, bf16[128,1024]{1,0:T(8,128)(2,1)}, u32[]{:S(2)}) copy-start(bf16[128,1024]{1,0:T(8,128)(2,1)} %gout_ref.1) | copy-start | bytes 786436
  6.3 0.9 %copy-start.5 = (f32[256,256]{1,0:T(8,128)S(1)}, f32[256,256]{1,0:T(8,128)}, u32[]{:S(2)}) copy-start(f32[256,256]{1,0:T(8,128)} %w2_ref.1) | copy-start | bytes 786436
  7.3 0.8 %copy-start.6 = (f32[32,256]{1,0:T(8,128)S(1)}, f32[32,256]{1,0:T(8,128)}, u32[]{:S(2)}) copy-start(f32[32,256]{1,0:T(8,128)} %w1_ref.1) | copy-start | bytes 98308
  8.0 0.8 %copy-start.7 = (f32[64,32]{1,0:T(8,128)S(1)}, f32[64,32]{1,0:T(8,128)}, u32[]{:S(2)}) copy-start(f32[64,32]{1,0:T(8,128)} %constant.6.clone.feat_ref) | copy-start | bytes 24580
  8.8 0.7 %copy-start.8 = (f32[32,64]{1,0:T(8,128)S(1)}, f32[32,64]{1,0:T(8,128)}, u32[]{:S(2)}) copy-start(f32[32,64]{1,0:T(8,128)} %constant.7.clone.featt_ref) | copy-start | bytes 24580
  9.5 0.7 %copy-start.9 = (f32[1024]{0:T(1024)S(1)}, f32[1024]{0:T(1024)}, u32[]{:S(2)}) copy-start(f32[1024]{0:T(1024)} %param.21) | copy-start | bytes 12292
  10.2 0.7 %copy-start.10 = (s32[1024]{0:T(1024)S(1)}, s32[1024]{0:T(1024)}, u32[]{:S(2)}) copy-start(s32[1024]{0:T(1024)} %param.22) | copy-start | bytes 12292
  10.9 0.7 %copy-start.11 = (f32[256]{0:T(256)S(1)}, f32[256]{0:T(256)}, u32[]{:S(2)}) copy-start(f32[256]{0:T(256)} %param.17) | copy-start | bytes 3076
  11.5 0.7 %copy-start.12 = (f32[256]{0:T(256)S(1)}, f32[256]{0:T(256)}, u32[]{:S(2)}) copy-start(f32[256]{0:T(256)} %param.19) | copy-start | bytes 3076
where the time goes:
time: 52.9 us; the launch traced here: 52.3 us
  Pallas kernels  35.2 us (67%)
  local copies, waits for them, and re-layouts  16.4 us (31%)
  between operations  0.67 us (1%)
    pallas_call x1, Pallas kernels, exchanged(): pl.pallas_call(functools.partial(exchange_kernel, (n, m, rows, width, win...  35.2 us
    unnamed x33, local copies, waits for them, and re-layouts  16.4 us

commit v1 on v0

--- a/solution.py
+++ b/solution.py
@@ -201,6 +201,7 @@
     )
 
 
+VMEM_LIMIT = 67_000_000
 MESH = pl.DeviceIdType.MESH
 
 
@@ -225,22 +226,31 @@
 
 
 def exchange_kernel(
-    sizes, x_ref, gate_ref, gout_ref, w1_ref, b1_ref, w2_ref, b2_ref, decay_ref, mask_ref,
-    feat_ref, featt_ref, table_hbm, ow_hbm,
+    sizes, x_hbm, gate_hbm, gout_hbm, w1_hbm, b1_hbm, w2_hbm, b2_hbm, decay_hbm, mask_hbm,
+    feat_hbm, featt_hbm, ow_hbm, table_hbm,
+    gi_out, gg_out, gw1_out, gb1_out, gw2_out, gb2_out, gow_out,
     gi_ref, gg_ref, gw1_ref, gb1_ref, gw2_ref, gb2_ref, gow_ref,
-    table, turned, ow, carried, xc, conv_in, taps, env, spec, tspec, prod, back, sums,
+    x_ref, gate_ref, gout_ref, w1_ref, b1_ref, w2_ref, b2_ref, decay_ref, mask_ref,
+    feat_ref, featt_ref, ow, table,
+    ow_hi, ow_lo, turned, carried, xc, conv_in, taps, env, spec, tspec, prod, back, sums,
     gts, gtall, units, send_sem, recv_sem, usend, urecv, local_sem,
+    store_sem,
 ):
     n, m, rows, width, window, period = sizes
     tokens = n * rows
     half = tokens // 2
     me = lax.axis_index("seq")
     mine = lax.axis_index("ch")
-    table_copy = pltpu.make_async_copy(table_hbm, table, local_sem.at[0])
-    table_copy.start()
-    ow_copy = pltpu.make_async_copy(ow_hbm, ow, local_sem.at[1])
-    ow_copy.start()
-    carried[...] = bf(gout_ref[...].astype(jnp.float32) * gate_ref[...].astype(jnp.float32))
+    loads = []
+    for at, (source, target) in enumerate((
+        (x_hbm, x_ref), (gate_hbm, gate_ref), (gout_hbm, gout_ref), (w1_hbm, w1_ref),
+        (b1_hbm, b1_ref), (w2_hbm, w2_ref), (b2_hbm, b2_ref), (decay_hbm, decay_ref),
+        (mask_hbm, mask_ref), (feat_hbm, feat_ref), (featt_hbm, featt_ref), (ow_hbm, ow),
+        (table_hbm, table),
+    )):
+        load = pltpu.make_async_copy(source, target, local_sem.at[at])
+        load.start()
+        loads.append(load)
     order = sorted(range(1, n), key=lambda step: -min(step, n - step))
     peers = {step: lax.rem(me + step, n) for step in order}
     others = {step: lax.rem(mine + step, m) for step in range(1, m)}
@@ -250,6 +260,9 @@
         pl.semaphore_signal(barrier, inc=1, device_id={"seq": peers[step]}, device_id_type=MESH)
     for step in range(1, m):
         pl.semaphore_signal(barrier, inc=1, device_id={"ch": others[step]}, device_id_type=MESH)
+    for load in loads[:3]:
+        load.wait()
+    carried[...] = bf(gout_ref[...].astype(jnp.float32) * gate_ref[...].astype(jnp.float32))
     pl.semaphore_wait(barrier, n + m - 2)
 
     own_rows = pl.ds(pl.multiple_of(me * rows, rows), rows)
@@ -275,13 +288,14 @@
     xc[own_rows, width : 2 * width] = carried[:, own_cols]
 
     full = lax.Precision.HIGHEST
+    for load in loads[3:]:
+        load.wait()
     pre_one = dot(feat_ref[...], w1_ref[...], precision=full) + b1_ref[...]
     h_one = jnp.sin(pre_one)
     slope_one = jnp.cos(pre_one)
     pre_two = dot(h_one, w2_ref[...], precision=full) + b2_ref[...]
     h_two = jnp.sin(pre_two)
     slope_two = jnp.cos(pre_two)
-    ow_copy.wait()
     base = dot(h_two, ow[:, own_cols], precision=full)
     decay = decay_ref[:, own_cols]
     lengths = mask_ref[:, own_cols]
@@ -290,7 +304,6 @@
         part = jnp.where(lag < lengths, jnp.exp(-decay * lag.astype(jnp.float32)), 0.0)
         env[pl.ds(block * period, period), :] = part
         taps[pl.ds(block * period, period), :] = bf(base * part)
-    table_copy.wait()
 
     @pl.loop(0, tokens // 256)
     def _(i):
@@ -298,7 +311,10 @@
         tspec[piece, :] = dot(table[piece, 0:window], taps[...])
         turned[:, piece] = table[piece, :].T
 
-    h_one_t = bf(h_one.T)
+    h_one_t = h_one.T
+    upper_ow = bf(ow[...])
+    ow_hi[...] = upper_ow
+    ow_lo[...] = bf(ow[...] - upper_ow.astype(jnp.float32))
     h_two_t = bf(h_two.T)
     for copy in arriving:
         copy.wait()
@@ -360,7 +376,9 @@
 
     for copy in gathering:
         copy.wait()
-    units[mine] = bf(dot(gtall[...], bf(ow[...]), ((1,), (1,))))
+    units[mine] = dot(gtall[...], ow_hi[...], ((1,), (1,))) + dot(
+        gtall[...], ow_lo[...], ((1,), (1,))
+    )
     crossing = []
     for step in range(1, m):
         copy = pltpu.make_async_remote_copy(
@@ -371,20 +389,56 @@
         copy.start()
         crossing.append(copy)
     gow_ref[...] = dot(h_two_t, gtall[...])
+    stores = []
+
+    def store(at, source, target):
+        copy = pltpu.make_async_copy(source, target, store_sem.at[at])
+        copy.start()
+        stores.append(copy)
+
+    store(0, gow_ref, gow_out)
     for copy in crossing:
         copy.wait()
-    unit = units[0].astype(jnp.float32)
+    unit = units[0]
     for other in range(1, m):
-        unit = unit + units[other].astype(jnp.float32)
+        unit = unit + units[other]
     grad_two = unit * slope_two
-    gw2_ref[...] = dot(h_one_t, bf(grad_two))
+    gw2_ref[...] = dot(h_one_t, grad_two, precision=full)
     gb2_ref[...] = jnp.sum(grad_two, axis=0, keepdims=True)
-    grad_one = dot(bf(grad_two), bf(w2_ref[...]), ((1,), (1,))) * slope_one
-    gw1_ref[...] = dot(bf(featt_ref[...]), bf(grad_one))
+    grad_one = dot(grad_two, w2_ref[...], ((1,), (1,)), full) * slope_one
+    gw1_ref[...] = dot(featt_ref[...], grad_one, precision=full)
     gb1_ref[...] = jnp.sum(grad_one, axis=0, keepdims=True)
+    for at, (source, target) in enumerate((
+        (gw2_ref, gw2_out), (gb2_ref, gb2_out), (gw1_ref, gw1_out), (gb1_ref, gb1_out)
+    )):
+        store(1 + at, source, target)
     for copy in returning:
         copy.wait()
+    store(5, gi_ref, gi_out)
     gg_ref[...] = bf(gout_ref[...].astype(jnp.float32) * conv_in[...].astype(jnp.float32))
+    store(6, gg_ref, gg_out)
+    for copy in stores:
+        copy.wait()
+
+
+def drain_kernel(*refs):
+    count = len(refs) // 3
+    load_sem, store_sem = refs[-2:]
+    loads = [
+        pltpu.make_async_copy(refs[at], refs[2 * count + at], load_sem.at[at])
+        for at in range(count)
+    ]
+    stores = [
+        pltpu.make_async_copy(refs[2 * count + at], refs[count + at], store_sem.at[at])
+        for at in range(count)
+    ]
+    for load in loads:
+        load.start()
+    for at in range(count):
+        loads[at].wait()
+        stores[at].start()
+    for copy in stores:
+        copy.wait()
 
 
 def exchanged(
@@ -404,42 +458,54 @@
     )
     features = np.concatenate([np.cos(angles), np.sin(angles)], axis=1).astype(np.float32)
     f32, b16 = jnp.float32, jnp.bfloat16
-    vmem = pl.BlockSpec(memory_space=pltpu.VMEM)
-    anywhere = pl.BlockSpec(memory_space=pl.ANY)
+    outside = pl.BlockSpec(memory_space=pltpu.HBM)
     shape = jax.ShapeDtypeStruct
     sem = pltpu.SemaphoreType.DMA
+    arrays = (
+        inputs, gate_values, grad_out, first_weight, first_bias[None], second_weight,
+        second_bias[None], decay_rates[None], mask_lengths[None],
+        jnp.asarray(features), jnp.asarray(features.T.copy()), out_weight,
+        jnp.asarray(packed_table(tokens), dtype=b16),
+    )
+    out_shapes = (
+        shape((rows, channels), b16), shape((rows, channels), b16),
+        shape((emb, units), f32), shape((1, units), f32),
+        shape((units, units), f32), shape((1, units), f32),
+        shape((units, channels), f32),
+    )
     outs = pl.pallas_call(
         functools.partial(exchange_kernel, (n, m, rows, width, window, period)),
-        out_shape=(
-            shape((rows, channels), b16), shape((rows, channels), b16),
-            shape((emb, units), f32), shape((1, units), f32),
-            shape((units, units), f32), shape((1, units), f32),
-            shape((units, channels), f32),
-        ),
-        in_specs=[vmem] * 11 + [anywhere] * 2,
-        out_specs=(vmem,) * 7,
+        out_shape=out_shapes,
+        in_specs=[outside] * 13,
+        out_specs=(outside,) * 7,
         scratch_shapes=[
-            pltpu.VMEM((tokens, tokens), b16), pltpu.VMEM((tokens, tokens), b16),
-            pltpu.VMEM((units, channels), f32), pltpu.VMEM((rows, channels), b16),
+            *[pltpu.VMEM(out.shape, out.dtype) for out in out_shapes],
+            *[pltpu.VMEM(array.shape, array.dtype) for array in arrays],
+            pltpu.VMEM((units, channels), b16), pltpu.VMEM((units, channels), b16),
+            pltpu.VMEM((tokens, tokens), b16), pltpu.VMEM((rows, channels), b16),
             pltpu.VMEM((tokens, 2 * width), b16), pltpu.VMEM((rows, channels), b16),
             pltpu.VMEM((window, width), b16), pltpu.VMEM((window, width), f32),
             pltpu.VMEM((tokens, 2 * width), f32), pltpu.VMEM((tokens, width), f32),
             pltpu.VMEM((tokens, 3 * width), b16), pltpu.VMEM((tokens, 2 * width), b16),
             pltpu.VMEM((window, width), f32),
             pltpu.VMEM((period, width), b16), pltpu.VMEM((period, channels), b16),
-            pltpu.VMEM((m, period, units), b16),
-            sem((5, n)), sem((5, n)), sem((m,)), sem((m,)), sem((2,)),
+            pltpu.VMEM((m, period, units), f32),
+            sem((5, n)), sem((5, n)), sem((m,)), sem((m,)), sem((13,)), sem((7,)),
         ],
         compiler_params=pltpu.CompilerParams(
-            collective_id=0, has_side_effects=True, vmem_limit_bytes=48 * 1024 * 1024
+            collective_id=0, has_side_effects=True, vmem_limit_bytes=VMEM_LIMIT
         ),
         name="exchange",
-    )(
-        inputs, gate_values, grad_out, first_weight, first_bias[None], second_weight,
-        second_bias[None], decay_rates[None], mask_lengths[None],
-        jnp.asarray(features), jnp.asarray(features.T.copy()),
-        jnp.asarray(packed_table(tokens), dtype=b16), out_weight,
-    )
+    )(*arrays)
+    outs = pl.pallas_call(
+        drain_kernel,
+        out_shape=out_shapes,
+        in_specs=[outside] * 7,
+        out_specs=(outside,) * 7,
+        scratch_shapes=[*[pltpu.VMEM(out.shape, out.dtype) for out in out_shapes], sem((7,)), sem((7,))],
+        compiler_params=pltpu.CompilerParams(vmem_limit_bytes=VMEM_LIMIT),
+        name="drain",
+    )(*outs)
     grad_in, gates, gw1, gb1, gw2, gb2, gow = outs
     return grad_in, gates, gw1, gb1[0], gw2, gb2[0], gow
 

time: 52.9 us -> 39.3 us (0.74)
  local copies, waits for them, and re-layouts: 16.4 us -> 0 us
  Pallas kernels: 35.2 us -> 38.5 us
    unnamed x33 -> x0, local copies, waits for them, and re-layouts: 16.4 us -> none
    pallas_call x0 -> x1, Pallas kernels: none -> 2.59 us  [exchanged(): pl.pallas_call(drain_kernel, out_shape=out_shapes, in_specs=[outside] * 7...]
    pallas_call x1, Pallas kernels: 35.2 us -> 35.9 us  [exchanged(): pl.pallas_call(functools.partial(exchange_kernel, (n, m, rows, width, win...]
where the time goes in v1:
time: 39.3 us; the launch traced here: 39.2 us
  Pallas kernels  38.5 us (98%)
  between operations  0.64 us (2%)
    pallas_call x1, Pallas kernels, exchanged(): pl.pallas_call(functools.partial(exchange_kernel, (n, m, rows, width, win...  35.9 us
    pallas_call x1, Pallas kernels, exchanged(): pl.pallas_call(drain_kernel, out_shape=out_shapes, in_specs=[outside] * 7...  2.59 us

profile of v1, /device:TPU:0, one launch (start us, length us, event | category | flops | bytes accessed | tf_op | source)
XLA Modules:
  0.0 39.2 jit_solution(12351096805739293853)
XLA Ops:
  0.6 35.9 %exchange.1 = (bf16[128,1024]{1,0:T(8,128)(2,1)}, bf16[128,1024]{1,0:T(8,128)(2,1)}, f32[32,256]{1,0:T(8,128)}, f32[1,256]{1,0:T(1,128)}, f32[256,256]{1,0:T(8,1...) custom-call(bf16[128,1024]{1,0:T(8,128)(2,1)} %x_hbm.1, bf16[128,1024]{1,0:T(8,128)(2,1)} %gate_hbm.1, ...), custom_call_target="tpu_custom_call" | custom-call | tf_op jit(solution)/shard_map/exchange/pallas_call | solution.py:476
  36.6 2.6 %drain.1 = (bf16[128,1024]{1,0:T(8,128)(2,1)}, bf16[128,1024]{1,0:T(8,128)(2,1)}, f32[32,256]{1,0:T(8,128)}, f32[1,256]{1,0:T(1,128)}, f32[256,256]{1,0:T(8,128)...) custom-call(bf16[128,1024]{1,0:T(8,128)(2,1)} %get-tuple-element.21.refs_0_, bf16[128,1024]{1,0:T(8,128)(2,1)} %get-tuple-element.22.refs_1_, ...), custom_call_target="tpu_custom_call" | custom-call | tf_op jit(solution)/shard_map/drain/pallas_call | solution.py:500
